TPU v7x, 512 devices: a whole 4x4x16 slice. The times are simulated.
512 devices in a mesh: dp: 32 (over z, core), seq: 16 (over y, x).
Axes of the slice: x: 4, y: 4, z: 16, core: 2. Of those that a mesh axis runs over, the one named last changes fastest.
Arguments:
- features: bfloat16 [32, 3072, 1024], P('dp', 'seq'), may hold values from -18 to 18
- qkv_weight: bfloat16 [1024, 3072], P('dp'), may hold values from -1 to 1
- cotangent: bfloat16 [32, 3072, 1024], P('dp', 'seq'), may hold values from -6 to 6
- node_order: int32 [32, 3072], P('dp'), may hold values from 0 to 3071, as said below
- blocks: int32 [32, 48, 8], P('dp'), may hold values from 0 to 47, as said below
- counts: int32 [32, 48], P('dp'), may hold values from 1 to 8, as said below
Outputs:
- attended: bfloat16 [32, 3072, 1024], P('dp', 'seq')
- grad_features: bfloat16 [32, 3072, 1024], P('dp', 'seq')
- grad_weight: float32 [1024, 3072], P('dp', 'seq')
Inputs may be any that keep to these rules, and one draw needn't show every extreme that they name: Every row of node_order lists each node of the subgraph once. blocks[g, c, 0] is c, and the 8 entries of a row are distinct clusters; slots at or beyond counts[g, c] are unused. `counts`: every subgraph has a cluster with all 8 slots live.
All inputs are finite; a program needn't handle non-finite values.
Results may differ from a plain program's by a relative error of at most 0.03.
Values may be sent and summed in bfloat16 or wider, within the bound.
No kernel may reach another device: no remote copies, remote signals or barrier semaphores. Data moves between devices by JAX's collectives and lax.ppermute only.
A program may use at most 128 MiB of HBM per device.

v0:
```python
import math
import jax
import jax.numpy as jnp
from jax import lax
from jax.sharding import PartitionSpec as P

HEADS = 16
HD = 64


def attend(query, key_in, value, grad_out, blocks, counts):
    cluster_count, slot_count = blocks.shape
    node_count, head_width = query.shape
    block_rows = node_count // cluster_count
    in_group = math.gcd(cluster_count, 8)
    runs_total = cluster_count // in_group
    score_scale = 1.0 / math.sqrt(head_width)
    key_blocks = key_in.reshape(cluster_count, block_rows, head_width)
    value_blocks = value.reshape(cluster_count, block_rows, head_width)
    inputs_all = (
        query.reshape(runs_total, in_group, block_rows, head_width),
        grad_out.reshape(runs_total, in_group, block_rows, head_width),
        blocks.reshape(runs_total, in_group, slot_count),
        counts.reshape(runs_total, in_group),
    )

    def group_step(totals, inputs_now):
        grad_key, grad_value = totals
        query_block, grad_block, block_ids, live_count = inputs_now
        key_rows = key_blocks[block_ids].reshape(in_group, slot_count * block_rows, head_width)
        value_rows = value_blocks[block_ids].reshape(in_group, slot_count * block_rows, head_width)
        is_live = jnp.repeat(
            jnp.arange(slot_count)[None, :] < live_count[:, None], block_rows, axis=1
        )[:, None, :]
        scores = (
            jnp.einsum("cqe,cke->cqk", query_block, key_rows, preferred_element_type=jnp.float32)
            * score_scale
        )
        scores = jnp.where(is_live, scores, -1e30)
        row_max = jnp.max(scores, axis=-1, keepdims=True)
        raw_weights = jnp.where(is_live, jnp.exp(scores - row_max), 0.0)
        attn_weights = raw_weights / jnp.sum(raw_weights, axis=-1, keepdims=True)
        attn_low = attn_weights.astype(jnp.bfloat16)
        output_blk = jnp.einsum(
            "cqk,cke->cqe", attn_low, value_rows, preferred_element_type=jnp.float32
        ).astype(jnp.bfloat16)
        grad_weights = jnp.einsum(
            "cqe,cke->cqk", grad_block, value_rows, preferred_element_type=jnp.float32
        )
        row_dot = jnp.sum(attn_weights * grad_weights, axis=-1, keepdims=True)
        grad_scores = (attn_weights * (grad_weights - row_dot) * score_scale).astype(jnp.bfloat16)
        grad_query = jnp.einsum(
            "cqk,cke->cqe", grad_scores, key_rows, preferred_element_type=jnp.float32
        ).astype(jnp.bfloat16)
        key_terms = jnp.einsum(
            "cqk,cqe->cke", grad_scores, query_block, preferred_element_type=jnp.float32
        )
        value_terms = jnp.einsum(
            "cqk,cqe->cke", attn_low, grad_block, preferred_element_type=jnp.float32
        )
        grad_key = grad_key.at[block_ids].add(
            key_terms.reshape(in_group, slot_count, block_rows, head_width)
        )
        grad_value = grad_value.at[block_ids].add(
            value_terms.reshape(in_group, slot_count, block_rows, head_width)
        )
        return ((grad_key, grad_value), (output_blk, grad_query))

    empty_sum = jnp.zeros((cluster_count, block_rows, head_width), jnp.float32)
    (grad_key, grad_value), (output_all, grad_query) = lax.scan(
        group_step, (empty_sum, empty_sum), inputs_all
    )
    return (
        output_all.reshape(node_count, head_width),
        grad_query.reshape(node_count, head_width),
        grad_key.reshape(node_count, head_width).astype(jnp.bfloat16),
        grad_value.reshape(node_count, head_width).astype(jnp.bfloat16),
    )


def per_device(features, qkv_weight, cotangent, node_order, blocks, counts):
    local_rows = features.shape[1]
    model_width = features.shape[2]
    heads_local = HEADS // lax.axis_size("seq")
    three_width = 3 * HD
    node_feats = features[0]
    cot_heads = cotangent[0].reshape(local_rows, HEADS, HD)
    weights_all = lax.all_gather(qkv_weight, "dp", axis=0, tiled=True)
    node_all = lax.all_gather(node_feats, "seq", axis=0, tiled=True)
    node_count = node_all.shape[0]
    projected = jnp.dot(node_feats, weights_all, preferred_element_type=jnp.float32).astype(
        jnp.bfloat16
    )
    projected = projected.reshape(local_rows, HEADS, three_width)
    head_qkv, head_cot = (
        lax.all_to_all(projected, "seq", split_axis=1, concat_axis=0, tiled=True),
        lax.all_to_all(cot_heads, "seq", split_axis=1, concat_axis=0, tiled=True),
    )
    graph_order = node_order[0]
    inverse = (
        jnp.zeros((node_count,), jnp.int32)
        .at[graph_order]
        .set(jnp.arange(node_count, dtype=jnp.int32))
    )
    sorted_qkv = head_qkv[graph_order]
    sorted_cot = head_cot[graph_order]
    output_all, grad_query, grad_key, grad_value = jax.vmap(
        attend, in_axes=(1, 1, 1, 1, None, None), out_axes=1
    )(
        sorted_qkv[:, :, :HD],
        sorted_qkv[:, :, HD : 2 * HD],
        sorted_qkv[:, :, 2 * HD :],
        sorted_cot,
        blocks[0],
        counts[0],
    )
    grad_heads = jnp.concatenate([grad_query, grad_key, grad_value], axis=-1)[inverse]
    output_nodes = output_all[inverse]
    output_back, grad_back = (
        lax.all_to_all(output_nodes, "seq", split_axis=0, concat_axis=1, tiled=True),
        lax.all_to_all(grad_heads, "seq", split_axis=0, concat_axis=1, tiled=True),
    )
    attended = output_back.reshape(1, local_rows, model_width)
    grad_local = grad_back.reshape(local_rows, 3 * model_width)
    grad_feats = lax.dot_general(
        grad_local, weights_all, (((1,), (1,)), ((), ())), preferred_element_type=jnp.float32
    )
    grad_features = grad_feats.astype(jnp.bfloat16).reshape(1, local_rows, model_width)
    head_grads = grad_heads.reshape(node_count, heads_local * three_width)
    grad_weight = lax.psum_scatter(
        lax.dot_general(
            node_all, head_grads, (((0,), (0,)), ((), ())), preferred_element_type=jnp.float32
        ).astype(jnp.bfloat16),
        "dp",
        scatter_dimension=0,
        tiled=True,
    ).astype(jnp.float32)
    return (attended, grad_features, grad_weight)


def solution(mesh):
    return jax.shard_map(
        per_device,
        mesh=mesh,
        in_specs=(
            P("dp", "seq", None),
            P("dp", None),
            P("dp", "seq", None),
            P("dp", None),
            P("dp", None, None),
            P("dp", None),
        ),
        out_specs=(P("dp", "seq", None), P("dp", "seq", None), P("dp", "seq")),
        check_vma=False,
    )
```

profile of v0, /device:TPU:8, one launch (start us, length us, event | category | flops | bytes accessed | tf_op | source)
XLA Modules:
  0.0 628.1 jit_solution(6024842970168261089)
XLA Ops:
  9.9 9.2 %all-to-all-start.1 = ((bf16[192,16,64]{0,2,1:T(8,128)(2,1)}), bf16[192,16,64]{0,2,1:T(8,128)(2,1)S(1)}, u32[]{:S(2)}, u32[]{:S(2)}) async-start(bf16[192,16,64]{0,2,1:T(8,128)(2,1)} %bitcast.27), calls=%async_computation.1 | async-start | bytes 1048576 | tf_op jit(solution)/shard_map/all_to_all | solution.py:97
  21.2 70.2 %all-gather.4.cloned.1.call-done = bf16[1024,3072]{1,0:T(8,128)(2,1)} async-done(((bf16[32,3072]{1,0:T(8,128)(2,1)}), bf16[1024,3072]{1,0:T(8,128)(2,1)}) %all-gather.4.cloned.1.call-update) | async-done | bytes 6291472 | tf_op jit(solution)/shard_map/all_gather | solution.py:88
  101.5 7.4 %all-to-all-start = ((bf16[192,16,192]{2,0,1:T(8,128)(2,1)}), bf16[192,16,192]{2,0,1:T(8,128)(2,1)S(1)}, u32[]{:S(2)}, u32[]{:S(2)}) async-start(bf16[192,16,192]{2,0,1:T(8,128)(2,1)} %copy.93), calls=%async_computation | async-start | bytes 3145728 | tf_op jit(solution)/shard_map/all_to_all | solution.py:96
  108.9 12.0 %scatter_custom_fusion.2 = s32[3072]{0:T(1024)S(1)} fusion(s32[3072]{0:T(1024)S(1)} %bitcast.182, s32[3072]{0:T(1024)S(1)} %iota.7, s32[]{:T(128)} %copy.139), kind=kCustom, calls=%fused_computation.71 | custom fusion | bytes 12292 | tf_op jit(solution)/shard_map/scatter | solution.py:103
  121.3 11.4 %gather_fusion.3 = bf16[3072,64]{1,0:T(8,128)(2,1)} fusion(bf16[3072,64]{1,0:T(8,128)(2,1)S(1)} %bitcast.161, s32[3072]{0:T(1024)S(1)} %broadcast_clamp_fusion), kind=kCustom, calls=%fused_computation.3 | custom fusion | bytes 798720 | tf_op jit(solution)/shard_map/gather | solution.py:106
  137.2 11.1 %gather_fusion.2 = bf16[3072,192]{1,0:T(8,128)(2,1)S(1)} fusion(bf16[3072,192]{1,0:T(8,128)(2,1)S(1)} %bitcast.152, s32[3072]{0:T(1024)S(1)} %broadcast_clamp_fusion), kind=kCustom, calls=%fused_computation.2 | custom fusion | bytes 2371584 | tf_op jit(solution)/shard_map/gather | solution.py:105
  150.4 286.3 %while.16 = (s32[]{:T(128)}, f32[1,48,64,64]{3,2,1,0:T(8,128)S(1)}, f32[1,48,64,64]{3,2,1,0:T(8,128)S(1)}, bf16[6,1,8,64,64]{4,3,2,1,0:T(8,128)(2,1)}, bf16[6,1,...) while((s32[]{:T(128)}, f32[1,48,64,64]{3,2,1,0:T(8,128)S(1)}, ...), condition=%wide.region_6.7_spmd, body=%wide.region_0.6_spmd.sunk | while | flops 209000192 | bytes 36499064 | solution.py:70
  173.6 7.0 %scatter_fusion.1 = f32[48,64,64]{2,1,0:T(8,128)S(1)} fusion(f32[48,64,64]{2,1,0:T(8,128)S(1)} %bitcast.155, s32[64]{0:T(128)S(1)} %reshape.343, f32[64,64,64]{2,1,0:T(8,128)} %bitcast.163), kind=kCustom, calls=%fused_computation.7.clone.1 | custom fusion | flops 262144 | bytes 3145984 | tf_op jit(solution)/shard_map/vmap()/while/body/eval_jaxpr/scatter-add | solution.py:64
  180.6 7.0 %fusion.110 = f32[8,512,64]{2,1,0:T(8,128)} fusion(f32[8,64,512]{2,1,0:T(8,128)} %fusion.106, bf16[6,1,8,64,64]{4,3,2,1,0:T(8,128)(2,1)} %get-tuple-element.266, s32[]{:T(128)} %get-tuple-element.247, f32[8,64,512]{2,1,0:T(8,128)} %get-tuple-element.233, f32[8,64]{1,0:T(8,128)S(1)} %get-tuple-element.234), kind=kOutput, calls=%fused_computation.26.clone.1 | convolution fusion | flops 35390464 | bytes 5382656 | tf_op jit(solution)/shard_map/vmap()/while/body/eval_jaxpr/reshape | solution.py:62
  187.7 7.0 %scatter_fusion = f32[48,64,64]{2,1,0:T(8,128)S(1)} fusion(f32[48,64,64]{2,1,0:T(8,128)S(1)} %bitcast.153, s32[64]{0:T(128)S(1)} %reshape.343, f32[64,64,64]{2,1,0:T(8,128)} %bitcast.162), kind=kCustom, calls=%fused_computation.6.clone.1 | custom fusion | flops 262144 | bytes 3145984 | tf_op jit(solution)/shard_map/vmap()/while/body/eval_jaxpr/scatter-add | solution.py:61
  221.3 7.0 %scatter_fusion.1 = f32[48,64,64]{2,1,0:T(8,128)S(1)} fusion(f32[48,64,64]{2,1,0:T(8,128)S(1)} %bitcast.155, s32[64]{0:T(128)S(1)} %reshape.343, f32[64,64,64]{2,1,0:T(8,128)} %bitcast.163), kind=kCustom, calls=%fused_computation.7.clone.1 | custom fusion | flops 262144 | bytes 3145984 | tf_op jit(solution)/shard_map/vmap()/while/body/eval_jaxpr/scatter-add | solution.py:64
  228.3 7.0 %fusion.110 = f32[8,512,64]{2,1,0:T(8,128)} fusion(f32[8,64,512]{2,1,0:T(8,128)} %fusion.106, bf16[6,1,8,64,64]{4,3,2,1,0:T(8,128)(2,1)} %get-tuple-element.266, s32[]{:T(128)} %get-tuple-element.247, f32[8,64,512]{2,1,0:T(8,128)} %get-tuple-element.233, f32[8,64]{1,0:T(8,128)S(1)} %get-tuple-element.234), kind=kOutput, calls=%fused_computation.26.clone.1 | convolution fusion | flops 35390464 | bytes 5382656 | tf_op jit(solution)/shard_map/vmap()/while/body/eval_jaxpr/reshape | solution.py:62
  235.4 7.0 %scatter_fusion = f32[48,64,64]{2,1,0:T(8,128)S(1)} fusion(f32[48,64,64]{2,1,0:T(8,128)S(1)} %bitcast.153, s32[64]{0:T(128)S(1)} %reshape.343, f32[64,64,64]{2,1,0:T(8,128)} %bitcast.162), kind=kCustom, calls=%fused_computation.6.clone.1 | custom fusion | flops 262144 | bytes 3145984 | tf_op jit(solution)/shard_map/vmap()/while/body/eval_jaxpr/scatter-add | solution.py:61
  269.0 7.0 %scatter_fusion.1 = f32[48,64,64]{2,1,0:T(8,128)S(1)} fusion(f32[48,64,64]{2,1,0:T(8,128)S(1)} %bitcast.155, s32[64]{0:T(128)S(1)} %reshape.343, f32[64,64,64]{2,1,0:T(8,128)} %bitcast.163), kind=kCustom, calls=%fused_computation.7.clone.1 | custom fusion | flops 262144 | bytes 3145984 | tf_op jit(solution)/shard_map/vmap()/while/body/eval_jaxpr/scatter-add | solution.py:64
  276.0 7.0 %fusion.110 = f32[8,512,64]{2,1,0:T(8,128)} fusion(f32[8,64,512]{2,1,0:T(8,128)} %fusion.106, bf16[6,1,8,64,64]{4,3,2,1,0:T(8,128)(2,1)} %get-tuple-element.266, s32[]{:T(128)} %get-tuple-element.247, f32[8,64,512]{2,1,0:T(8,128)} %get-tuple-element.233, f32[8,64]{1,0:T(8,128)S(1)} %get-tuple-element.234), kind=kOutput, calls=%fused_computation.26.clone.1 | convolution fusion | flops 35390464 | bytes 5382656 | tf_op jit(solution)/shard_map/vmap()/while/body/eval_jaxpr/reshape | solution.py:62
  283.1 7.0 %scatter_fusion = f32[48,64,64]{2,1,0:T(8,128)S(1)} fusion(f32[48,64,64]{2,1,0:T(8,128)S(1)} %bitcast.153, s32[64]{0:T(128)S(1)} %reshape.343, f32[64,64,64]{2,1,0:T(8,128)} %bitcast.162), kind=kCustom, calls=%fused_computation.6.clone.1 | custom fusion | flops 262144 | bytes 3145984 | tf_op jit(solution)/shard_map/vmap()/while/body/eval_jaxpr/scatter-add | solution.py:61
  316.7 7.0 %scatter_fusion.1 = f32[48,64,64]{2,1,0:T(8,128)S(1)} fusion(f32[48,64,64]{2,1,0:T(8,128)S(1)} %bitcast.155, s32[64]{0:T(128)S(1)} %reshape.343, f32[64,64,64]{2,1,0:T(8,128)} %bitcast.163), kind=kCustom, calls=%fused_computation.7.clone.1 | custom fusion | flops 262144 | bytes 3145984 | tf_op jit(solution)/shard_map/vmap()/while/body/eval_jaxpr/scatter-add | solution.py:64
  323.8 7.0 %fusion.110 = f32[8,512,64]{2,1,0:T(8,128)} fusion(f32[8,64,512]{2,1,0:T(8,128)} %fusion.106, bf16[6,1,8,64,64]{4,3,2,1,0:T(8,128)(2,1)} %get-tuple-element.266, s32[]{:T(128)} %get-tuple-element.247, f32[8,64,512]{2,1,0:T(8,128)} %get-tuple-element.233, f32[8,64]{1,0:T(8,128)S(1)} %get-tuple-element.234), kind=kOutput, calls=%fused_computation.26.clone.1 | convolution fusion | flops 35390464 | bytes 5382656 | tf_op jit(solution)/shard_map/vmap()/while/body/eval_jaxpr/reshape | solution.py:62
  330.8 7.0 %scatter_fusion = f32[48,64,64]{2,1,0:T(8,128)S(1)} fusion(f32[48,64,64]{2,1,0:T(8,128)S(1)} %bitcast.153, s32[64]{0:T(128)S(1)} %reshape.343, f32[64,64,64]{2,1,0:T(8,128)} %bitcast.162), kind=kCustom, calls=%fused_computation.6.clone.1 | custom fusion | flops 262144 | bytes 3145984 | tf_op jit(solution)/shard_map/vmap()/while/body/eval_jaxpr/scatter-add | solution.py:61
  354.2 6.0 fusion.113
  364.4 7.0 %scatter_fusion.1 = f32[48,64,64]{2,1,0:T(8,128)S(1)} fusion(f32[48,64,64]{2,1,0:T(8,128)S(1)} %bitcast.155, s32[64]{0:T(128)S(1)} %reshape.343, f32[64,64,64]{2,1,0:T(8,128)} %bitcast.163), kind=kCustom, calls=%fused_computation.7.clone.1 | custom fusion | flops 262144 | bytes 3145984 | tf_op jit(solution)/shard_map/vmap()/while/body/eval_jaxpr/scatter-add | solution.py:64
  371.5 7.0 %fusion.110 = f32[8,512,64]{2,1,0:T(8,128)} fusion(f32[8,64,512]{2,1,0:T(8,128)} %fusion.106, bf16[6,1,8,64,64]{4,3,2,1,0:T(8,128)(2,1)} %get-tuple-element.266, s32[]{:T(128)} %get-tuple-element.247, f32[8,64,512]{2,1,0:T(8,128)} %get-tuple-element.233, f32[8,64]{1,0:T(8,128)S(1)} %get-tuple-element.234), kind=kOutput, calls=%fused_computation.26.clone.1 | convolution fusion | flops 35390464 | bytes 5382656 | tf_op jit(solution)/shard_map/vmap()/while/body/eval_jaxpr/reshape | solution.py:62
  378.5 7.0 %scatter_fusion = f32[48,64,64]{2,1,0:T(8,128)S(1)} fusion(f32[48,64,64]{2,1,0:T(8,128)S(1)} %bitcast.153, s32[64]{0:T(128)S(1)} %reshape.343, f32[64,64,64]{2,1,0:T(8,128)} %bitcast.162), kind=kCustom, calls=%fused_computation.6.clone.1 | custom fusion | flops 262144 | bytes 3145984 | tf_op jit(solution)/shard_map/vmap()/while/body/eval_jaxpr/scatter-add | solution.py:61
  412.2 7.0 %scatter_fusion.1 = f32[48,64,64]{2,1,0:T(8,128)S(1)} fusion(f32[48,64,64]{2,1,0:T(8,128)S(1)} %bitcast.155, s32[64]{0:T(128)S(1)} %reshape.343, f32[64,64,64]{2,1,0:T(8,128)} %bitcast.163), kind=kCustom, calls=%fused_computation.7.clone.1 | custom fusion | flops 262144 | bytes 3145984 | tf_op jit(solution)/shard_map/vmap()/while/body/eval_jaxpr/scatter-add | solution.py:64
  419.2 7.0 %fusion.110 = f32[8,512,64]{2,1,0:T(8,128)} fusion(f32[8,64,512]{2,1,0:T(8,128)} %fusion.106, bf16[6,1,8,64,64]{4,3,2,1,0:T(8,128)(2,1)} %get-tuple-element.266, s32[]{:T(128)} %get-tuple-element.247, f32[8,64,512]{2,1,0:T(8,128)} %get-tuple-element.233, f32[8,64]{1,0:T(8,128)S(1)} %get-tuple-element.234), kind=kOutput, calls=%fused_computation.26.clone.1 | convolution fusion | flops 35390464 | bytes 5382656 | tf_op jit(solution)/shard_map/vmap()/while/body/eval_jaxpr/reshape | solution.py:62
  426.2 7.0 %scatter_fusion = f32[48,64,64]{2,1,0:T(8,128)S(1)} fusion(f32[48,64,64]{2,1,0:T(8,128)S(1)} %bitcast.153, s32[64]{0:T(128)S(1)} %reshape.343, f32[64,64,64]{2,1,0:T(8,128)} %bitcast.162), kind=kCustom, calls=%fused_computation.6.clone.1 | custom fusion | flops 262144 | bytes 3145984 | tf_op jit(solution)/shard_map/vmap()/while/body/eval_jaxpr/scatter-add | solution.py:61
  438.9 9.2 %gather_fusion.4 = bf16[3072,64]{1,0:T(8,128)(2,1)S(1)} fusion(bf16[3072,64]{1,0:T(8,128)(2,1)S(1)} %bitcast.164, s32[3072]{0:T(1024)S(1)} %fusion.52), kind=kCustom, calls=%fused_computation.4 | custom fusion | bytes 798720 | tf_op jit(solution)/shard_map/gather | solution.py:118
  459.1 11.1 %gather_fusion.5 = bf16[3072,192]{1,0:T(8,128)(2,1)S(1)} fusion(bf16[3072,192]{1,0:T(8,128)(2,1)S(1)} %maximum_bitcast_fusion, s32[3072]{0:T(1024)S(1)} %fusion.52), kind=kCustom, calls=%fused_computation.5 | custom fusion | bytes 2371584 | tf_op jit(solution)/shard_map/gather | solution.py:117
  474.5 7.3 %all-to-all-start.3 = ((bf16[16,2,18432]{2,1,0:T(2,128)(2,1)}), bf16[16,2,18432]{2,1,0:T(2,128)(2,1)}, u32[]{:S(2)}, u32[]{:S(2)}) async-start(bf16[16,2,18432]{2,1,0:T(2,128)(2,1)} %reshape.324), calls=%async_computation.3 | async-start | bytes 2359296 | tf_op jit(solution)/shard_map/all_to_all | solution.py:121
  491.1 101.6 %reduce-scatter.4.cloned.1.call-done = bf16[32,192]{1,0:T(8,128)(2,1)} async-done(((bf16[1024,192]{1,0:T(8,128)(2,1)}), bf16[32,192]{1,0:T(8,128)(2,1)}) %reduce-scatter.4.cloned.1.call-update) | async-done | bytes 12304
  594.2 8.4 %reshape.325 = bf16[3072,1,192]{2,1,0:T(2,128)(2,1)S(1)} reshape(bf16[16,2,18432]{2,1,0:T(2,128)(2,1)} %all-to-all-done.3) | data formatting | bytes 2359296
  602.6 6.2 copy.102
  (164 shorter events, 216.7 us)
Async XLA Ops:
  7.2 84.3 %copy-start.3 = (bf16[1,192,1024]{2,1,0:T(8,128)(2,1)S(1)}, bf16[1,192,1024]{2,1,0:T(8,128)(2,1)}, u32[]{:S(2)}) copy-start(bf16[1,192,1024]{2,1,0:T(8,128)(2,1)} %param.8) | copy-start | bytes 1179652
  7.2 12.7 %copy-start.5 = (s32[1,48,8]{1,2,0:T(8,128)S(1)}, s32[1,48,8]{1,2,0:T(8,128)}, u32[]{:S(2)}) copy-start(s32[1,48,8]{1,2,0:T(8,128)} %param.12) | copy-start | bytes 4612
  7.2 13.3 %copy-start.6 = (s32[1,48]{1,0:T(1,128)S(1)}, s32[1,48]{1,0:T(1,128)}, u32[]{:S(2)}) copy-start(s32[1,48]{1,0:T(1,128)} %param.13) | copy-start | bytes 580
  7.2 84.3 %all-gather.4.cloned.1.call-start = ((), (), s32[]{:S(2)}) async-start(), calls=%async_computation.5 | async-start | bytes 6488064 | tf_op jit(solution)/shard_map/all_gather | solution.py:88
  9.9 91.6 %all-to-all-start.1 = ((bf16[192,16,64]{0,2,1:T(8,128)(2,1)}), bf16[192,16,64]{0,2,1:T(8,128)(2,1)S(1)}, u32[]{:S(2)}, u32[]{:S(2)}) async-start(bf16[192,16,64]{0,2,1:T(8,128)(2,1)} %bitcast.27), calls=%async_computation.1 | async-start | bytes 1048576 | tf_op jit(solution)/shard_map/all_to_all | solution.py:97
  19.1 462.7 %all-gather.6.cloned.1.call-start = ((), (), s32[]{:S(2)}) async-start(), calls=%async_computation.6 | async-start | bytes 6684672 | tf_op jit(solution)/shard_map/all_gather | solution.py:89
  101.5 7.4 %copy-start.4 = (s32[1,3072]{1,0:T(1,128)S(1)}, s32[1,3072]{1,0:T(1,128)}, u32[]{:S(2)}) copy-start(s32[1,3072]{1,0:T(1,128)} %param.11) | copy-start | bytes 36868
  101.5 35.7 %all-to-all-start = ((bf16[192,16,192]{2,0,1:T(8,128)(2,1)}), bf16[192,16,192]{2,0,1:T(8,128)(2,1)S(1)}, u32[]{:S(2)}, u32[]{:S(2)}) async-start(bf16[192,16,192]{2,0,1:T(8,128)(2,1)} %copy.93), calls=%async_computation | async-start | bytes 3145728 | tf_op jit(solution)/shard_map/all_to_all | solution.py:96
  155.4 1.0 copy-start
  203.2 1.0 copy-start
  250.9 1.0 copy-start
  298.6 1.0 copy-start
  346.3 1.0 copy-start
  394.0 1.0 copy-start
  437.8 1.1 copy-start.1
  448.6 8.6 %copy-start.2 = (bf16[1,48,64,64]{3,2,1,0:T(8,128)(2,1)S(1)}, bf16[1,48,64,64]{3,2,1,0:T(8,128)(2,1)}, u32[]{:S(2)}) copy-start(bf16[1,48,64,64]{3,2,1,0:T(8,128)(2,1)} %convert_element_type.62) | copy-start | bytes 1179652
  451.4 23.1 %all-to-all-start.2 = ((bf16[16,2,6144]{2,1,0:T(2,128)(2,1)}), bf16[16,2,6144]{2,1,0:T(2,128)(2,1)S(1)}, u32[]{:S(2)}, u32[]{:S(2)}) async-start(bf16[16,2,6144]{2,1,0:T(2,128)(2,1)} %reshape.322), calls=%async_computation.2 | async-start | bytes 786432 | tf_op jit(solution)/shard_map/all_to_all | solution.py:120
  474.5 119.7 %all-to-all-start.3 = ((bf16[16,2,18432]{2,1,0:T(2,128)(2,1)}), bf16[16,2,18432]{2,1,0:T(2,128)(2,1)}, u32[]{:S(2)}, u32[]{:S(2)}) async-start(bf16[16,2,18432]{2,1,0:T(2,128)(2,1)} %reshape.324), calls=%async_computation.3 | async-start | bytes 2359296 | tf_op jit(solution)/shard_map/all_to_all | solution.py:121
  481.7 110.9 %reduce-scatter.4.cloned.1.call-start = ((), (), s32[]{:S(2)}) async-start(), calls=%async_computation.7 | async-start | bytes 540672
Sparse Core Ops, SparseCore 0:
  10.2 81.2 all-gather.3
  94.5 83.8 all-gather.5
  487.2 105.4 reduce-scatter.3
where the time goes:
time: 633 us; the launch traced here: 628 us
  waiting for transfers between devices  178 us (28%)
  matrix products  168 us (27%)
  local copies, waits for them, and re-layouts  140 us (22%)
  other arithmetic  99 us (16%)
  starting transfers between devices  29.8 us (5%)
  between operations  14 us (2%)
    unnamed x4, waiting for transfers between devices  103 us
    all_gather x1, waiting for transfers between devices, per_device(): weights_all = lax.all_gather(qkv_weight, 'dp', axis=0, tiled=True)  70.2 us
    reshape x6, matrix products, group_step(): key_terms.reshape(in_group, slot_count, block_rows, head_width)  42.2 us
    scatter-add x6, other arithmetic, group_step(): grad_value.at[block_ids]  42 us
    scatter-add x6, other arithmetic, group_step(): grad_key.at[block_ids]  42 us
    dot_general x6, matrix products, group_step(): jnp.einsum('cqk,cke->cqe', grad_scores, key_rows, preferred_element_type=...  36 us
    reshape x6, matrix products, group_step(): value_terms.reshape(in_group, slot_count, block_rows, head_width)  25.7 us
    dot_general x6, matrix products, group_step(): jnp.einsum('cqk,cke->cqe', attn_low, value_rows, preferred_element_type=j...  21 us
  transfers between devices with their start and end apart: 7, of which 3 were waited for; matrix products, arithmetic and copies ran while one was open for 59% of the time, Pallas kernels for 0%

commit v1 on v0

--- a/solution.py
+++ b/solution.py
@@ -85,7 +85,8 @@
     three_width = 3 * HD
     node_feats = features[0]
     cot_heads = cotangent[0].reshape(local_rows, HEADS, HD)
-    weights_all = lax.all_gather(qkv_weight, "dp", axis=0, tiled=True)
+    copies = jnp.concatenate([qkv_weight] * lax.axis_size("dp"), axis=0)
+    weights_all = lax.all_to_all(copies, "dp", 0, 0, tiled=True)
     node_all = lax.all_gather(node_feats, "seq", axis=0, tiled=True)
     node_count = node_all.shape[0]
     projected = jnp.dot(node_feats, weights_all, preferred_element_type=jnp.float32).astype(

time: 633 us -> 861 us (1.36)
  the two profiles are of different devices: /device:TPU:8 before, /device:TPU:10 now
where the time goes in v1:
time: 861 us; the launch traced here: 856 us
  waiting for transfers between devices  373 us (43%)
  matrix products  168 us (20%)
  local copies, waits for them, and re-layouts  156 us (18%)
  other arithmetic  100 us (12%)
  starting transfers between devices  44.9 us (5%)
  between operations  14.5 us (2%)
    all_to_all x1, waiting for transfers between devices, per_device(): weights_all = lax.all_to_all(copies, 'dp', 0, 0, tiled=True)  272 us
    unnamed x3, waiting for transfers between devices  101 us
    reshape x6, matrix products, group_step(): key_terms.reshape(in_group, slot_count, block_rows, head_width)  42.2 us
    scatter-add x6, other arithmetic, group_step(): grad_value.at[block_ids]  42 us
    scatter-add x6, other arithmetic, group_step(): grad_key.at[block_ids]  42 us
    unnamed x60, local copies, waits for them, and re-layouts  36.4 us
    dot_general x6, matrix products, group_step(): jnp.einsum('cqk,cke->cqe', grad_scores, key_rows, preferred_element_type=...  36 us
    reshape x6, matrix products, group_step(): value_terms.reshape(in_group, slot_count, block_rows, head_width)  25.7 us
  transfers between devices with their start and end apart: 7, of which 2 were waited for; matrix products, arithmetic and copies ran while one was open for 43% of the time, Pallas kernels for 0%

profile of v1, /device:TPU:10, one launch (start us, length us, event | category | flops | bytes accessed | tf_op | source)
XLA Modules:
  0.0 856.4 jit_solution(18274275747433055854)
XLA Ops:
  25.4 15.7 %all-to-all-start = ((bf16[32,32,3072]{2,1,0:T(8,128)(2,1)}), bf16[32,32,3072]{2,1,0:T(8,128)(2,1)}, u32[]{:S(2)}, u32[]{:S(2)}) async-start(bf16[32,32,3072]{2,1,0:T(8,128)(2,1)} %bitcast.175), calls=%async_computation | async-start | bytes 12582912 | tf_op jit(solution)/shard_map/all_to_all | solution.py:89
  44.2 271.8 %all-to-all-done = bf16[32,32,3072]{2,1,0:T(8,128)(2,1)} async-done(((bf16[32,32,3072]{2,1,0:T(8,128)(2,1)}), bf16[32,32,3072]{2,1,0:T(8,128)(2,1)}, u32[]{:S(2)}, u32[]{:S(2)}) %all-to-all-start) | async-done | bytes 6291488 | tf_op jit(solution)/shard_map/all_to_all | solution.py:89
  316.1 7.4 all-to-all-start.2
  333.5 7.2 all-to-all-start.1
  340.7 12.0 %scatter_custom_fusion.2 = s32[3072]{0:T(1024)S(1)} fusion(s32[3072]{0:T(1024)S(1)} %bitcast.187, s32[3072]{0:T(1024)S(1)} %iota.7, s32[]{:T(128)} %copy.170), kind=kCustom, calls=%fused_computation.104 | custom fusion | bytes 12292 | tf_op jit(solution)/shard_map/scatter | solution.py:104
  353.1 11.4 %gather_fusion.3 = bf16[3072,64]{1,0:T(8,128)(2,1)} fusion(bf16[3072,64]{1,0:T(8,128)(2,1)S(1)} %bitcast.165, s32[3072]{0:T(1024)S(1)} %broadcast_clamp_fusion), kind=kCustom, calls=%fused_computation.3 | custom fusion | bytes 798720 | tf_op jit(solution)/shard_map/gather | solution.py:107
  364.6 11.1 %gather_fusion.2 = bf16[3072,192]{1,0:T(8,128)(2,1)S(1)} fusion(bf16[3072,192]{1,0:T(8,128)(2,1)S(1)} %bitcast.156, s32[3072]{0:T(1024)S(1)} %broadcast_clamp_fusion), kind=kCustom, calls=%fused_computation.2 | custom fusion | bytes 2371584 | tf_op jit(solution)/shard_map/gather | solution.py:106
  377.8 286.3 %while.16 = (s32[]{:T(128)}, f32[1,48,64,64]{3,2,1,0:T(8,128)S(1)}, f32[1,48,64,64]{3,2,1,0:T(8,128)S(1)}, bf16[6,1,8,64,64]{4,3,2,1,0:T(8,128)(2,1)}, bf16[6,1,...) while((s32[]{:T(128)}, f32[1,48,64,64]{3,2,1,0:T(8,128)S(1)}, ...), condition=%wide.region_6.7_spmd, body=%wide.region_0.6_spmd.sunk | while | flops 209000192 | bytes 36499064 | solution.py:70
  400.9 7.0 scatter_fusion.1
  408.0 7.0 fusion.111
  415.0 7.0 scatter_fusion
  448.7 7.0 scatter_fusion.1
  455.7 7.0 fusion.111
  462.7 7.0 scatter_fusion
  496.4 7.0 scatter_fusion.1
  503.4 7.0 fusion.111
  510.4 7.0 scatter_fusion
  544.1 7.0 scatter_fusion.1
  551.1 7.0 fusion.111
  558.1 7.0 scatter_fusion
  591.8 7.0 scatter_fusion.1
  598.8 7.0 fusion.111
  605.8 7.0 scatter_fusion
  639.5 7.0 scatter_fusion.1
  646.5 7.0 fusion.111
  653.5 7.0 scatter_fusion
  666.4 9.2 %gather_fusion.4 = bf16[3072,64]{1,0:T(8,128)(2,1)S(1)} fusion(bf16[3072,64]{1,0:T(8,128)(2,1)S(1)} %bitcast.168, s32[3072]{0:T(1024)S(1)} %fusion.53), kind=kCustom, calls=%fused_computation.4 | custom fusion | bytes 798720 | tf_op jit(solution)/shard_map/gather | solution.py:119
  678.8 7.2 all-to-all-start.3
  688.2 11.1 %gather_fusion.5 = bf16[3072,192]{1,0:T(8,128)(2,1)S(1)} fusion(bf16[3072,192]{1,0:T(8,128)(2,1)S(1)} %maximum_bitcast_fusion, s32[3072]{0:T(1024)S(1)} %fusion.53), kind=kCustom, calls=%fused_computation.5 | custom fusion | bytes 2371584 | tf_op jit(solution)/shard_map/gather | solution.py:118
  703.5 7.2 all-to-all-start.4
  720.1 100.6 %reduce-scatter.4.cloned.1.call-done = bf16[32,192]{1,0:T(8,128)(2,1)} async-done(((bf16[1024,192]{1,0:T(8,128)(2,1)}), bf16[32,192]{1,0:T(8,128)(2,1)}) %reduce-scatter.4.cloned.1.call-update) | async-done | bytes 12304
  822.2 8.4 reshape.327
  (201 shorter events, 235.2 us)
Async XLA Ops:
  7.2 15.2 %copy-start = (bf16[32,3072]{1,0:T(8,128)(2,1)S(1)}, bf16[32,3072]{1,0:T(8,128)(2,1)}, u32[]{:S(2)}) copy-start(bf16[32,3072]{1,0:T(8,128)(2,1)} %param.9) | copy-start | bytes 589828
  22.8 2.6 copy-start.3
  25.4 16.5 %copy-start.5 = (bf16[1,192,1024]{2,1,0:T(8,128)(2,1)S(1)}, bf16[1,192,1024]{2,1,0:T(8,128)(2,1)}, u32[]{:S(2)}) copy-start(bf16[1,192,1024]{2,1,0:T(8,128)(2,1)} %param.10) | copy-start | bytes 1179652
  25.4 17.5 %copy-start.8 = (s32[1,48,8]{1,2,0:T(8,128)S(1)}, s32[1,48,8]{1,2,0:T(8,128)}, u32[]{:S(2)}) copy-start(s32[1,48,8]{1,2,0:T(8,128)} %param.12) | copy-start | bytes 4612
  25.4 18.1 %copy-start.9 = (s32[1,48]{1,0:T(1,128)S(1)}, s32[1,48]{1,0:T(1,128)}, u32[]{:S(2)}) copy-start(s32[1,48]{1,0:T(1,128)} %param.13) | copy-start | bytes 580
  25.4 298.1 %copy-start.6 = (bf16[1,192,1024]{2,1,0:T(8,128)(2,1)S(1)}, bf16[1,192,1024]{2,1,0:T(8,128)(2,1)}, u32[]{:S(2)}) copy-start(bf16[1,192,1024]{2,1,0:T(8,128)(2,1)} %param.8) | copy-start | bytes 1179652
  25.4 290.7 %all-to-all-start = ((bf16[32,32,3072]{2,1,0:T(8,128)(2,1)}), bf16[32,32,3072]{2,1,0:T(8,128)(2,1)}, u32[]{:S(2)}, u32[]{:S(2)}) async-start(bf16[32,32,3072]{2,1,0:T(8,128)(2,1)} %bitcast.175), calls=%async_computation | async-start | bytes 12582912 | tf_op jit(solution)/shard_map/all_to_all | solution.py:89
  41.1 669.7 %all-gather.3.cloned.1.call-start = ((), (), s32[]{:S(2)}) async-start(), calls=%async_computation.6 | async-start | bytes 6684672 | tf_op jit(solution)/shard_map/all_gather | solution.py:90
  316.1 17.4 %all-to-all-start.2 = ((bf16[192,16,64]{0,2,1:T(8,128)(2,1)}), bf16[192,16,64]{0,2,1:T(8,128)(2,1)S(1)}, u32[]{:S(2)}, u32[]{:S(2)}) async-start(bf16[192,16,64]{0,2,1:T(8,128)(2,1)} %bitcast.30), calls=%async_computation.2 | async-start | bytes 1048576 | tf_op jit(solution)/shard_map/all_to_all | solution.py:98
  328.7 12.0 %copy-start.7 = (s32[1,3072]{1,0:T(1,128)S(1)}, s32[1,3072]{1,0:T(1,128)}, u32[]{:S(2)}) copy-start(s32[1,3072]{1,0:T(1,128)} %param.11) | copy-start | bytes 36868
  333.5 31.1 %all-to-all-start.1 = ((bf16[192,16,192]{2,0,1:T(8,128)(2,1)}), bf16[192,16,192]{2,0,1:T(8,128)(2,1)S(1)}, u32[]{:S(2)}, u32[]{:S(2)}) async-start(bf16[192,16,192]{2,0,1:T(8,128)(2,1)} %copy.93), calls=%async_computation.1 | async-start | bytes 3145728 | tf_op jit(solution)/shard_map/all_to_all | solution.py:97
  382.8 1.0 copy-start.1
  430.5 1.0 copy-start.1
  478.2 1.0 copy-start.1
  526.0 1.0 copy-start.1
  573.7 1.0 copy-start.1
  621.4 1.0 copy-start.1
  665.1 1.3 copy-start.2
  665.1 21.0 %copy-start.4 = (bf16[1,48,64,64]{3,2,1,0:T(8,128)(2,1)S(1)}, bf16[1,48,64,64]{3,2,1,0:T(8,128)(2,1)}, u32[]{:S(2)}) copy-start(bf16[1,48,64,64]{3,2,1,0:T(8,128)(2,1)} %convert_element_type.66) | copy-start | bytes 1179652
  678.8 24.7 %all-to-all-start.3 = ((bf16[16,2,6144]{2,1,0:T(2,128)(2,1)}), bf16[16,2,6144]{2,1,0:T(2,128)(2,1)S(1)}, u32[]{:S(2)}, u32[]{:S(2)}) async-start(bf16[16,2,6144]{2,1,0:T(2,128)(2,1)} %reshape.324), calls=%async_computation.3 | async-start | bytes 786432 | tf_op jit(solution)/shard_map/all_to_all | solution.py:121
  703.5 118.7 %all-to-all-start.4 = ((bf16[16,2,18432]{2,1,0:T(2,128)(2,1)}), bf16[16,2,18432]{2,1,0:T(2,128)(2,1)}, u32[]{:S(2)}, u32[]{:S(2)}) async-start(bf16[16,2,18432]{2,1,0:T(2,128)(2,1)} %reshape.326), calls=%async_computation.4 | async-start | bytes 2359296 | tf_op jit(solution)/shard_map/all_to_all | solution.py:122
  710.8 109.9 %reduce-scatter.4.cloned.1.call-start = ((), (), s32[]{:S(2)}) async-start(), calls=%async_computation.7 | async-start | bytes 540672
Sparse Core Ops, SparseCore 0:
  45.0 76.1 all-gather.2
  716.2 104.4 reduce-scatter.3
